TPU v7x, 256 devices: a whole 4x4x8 slice. The times are simulated.
256 devices in a mesh: ctx: 16 (over z_lo, y, core), heads: 16 (over z_hi, x).
Axes of the slice: x: 4, y: 4, z: 8 (z_hi: 4, z_lo: 2; z = z_hi * 2 + z_lo), core: 2. Of those that a mesh axis runs over, the one named last changes fastest.
Arguments:
- queries: bfloat16 [4096, 8192], P('ctx', 'heads'), may hold values from -48 to 48
- out_grad: bfloat16 [4096, 8192], P('ctx', 'heads'), may hold values from -48 to 48
- attn_out: bfloat16 [4096, 8192], P('ctx', 'heads'), may hold values from -6 to 6
- img_keys: bfloat16 [2048, 1024], P('ctx'), may hold values from -6 to 6
- img_values: bfloat16 [2048, 1024], P('ctx'), may hold values from -6 to 6
- key_weight: bfloat16 [8192, 1024], P('heads'), may hold values from -0.0625 to 0.0625
- value_weight: bfloat16 [8192, 1024], P('heads'), may hold values from -0.0625 to 0.0625
- proj_weight: bfloat16 [7680, 8192], P('heads'), may hold values from -0.0625 to 0.0625
- block_order: int32 [32], replicated, may hold values from 0 to 31, each once
- owner_counts: int32 [16], replicated, may hold values from 1 to 4, 32 in all
Outputs:
- d_query: bfloat16 [4096, 8192], P('ctx', 'heads')
- d_vision: bfloat16 [4096, 7680], P('ctx', 'heads')
Inputs may be any that keep to these rules, and one draw needn't show every extreme that they name: `block_order`: each of the 32 blocks appears once. `owner_counts`: the counts sum to 32; one owner has exactly 4.
All inputs are finite; a program needn't handle non-finite values.
Results may differ from a plain program's by a relative error of at most 0.015.
Values may be sent and summed in bfloat16 or wider, within the bound.
No kernel may reach another device: no remote copies, remote signals or barrier semaphores. Data moves between devices by JAX's collectives and lax.ppermute only.
A program may use at most 64 MiB of HBM per device.

v0:
```python
import jax
import jax.numpy as jnp
from jax import lax
from jax.sharding import PartitionSpec as P

KVH = 8
HD = 128
BR = 64
CAP = 4
CONTRACT_LAST = (((1,), (1,)), ((), ()))
CONTRACT_FIRST = (((0,), (0,)), ((), ()))


def from_everyone(array, axis):
    copies = jnp.broadcast_to(array, (lax.axis_size(axis), *array.shape))
    return lax.all_to_all(copies, axis, split_axis=0, concat_axis=0, tiled=True)


def laid_out(pieces, dim):
    shape = list(pieces.shape[1:])
    shape[dim] *= pieces.shape[0]
    return jnp.moveaxis(pieces, 0, dim).reshape(shape)


def gathered_copies(array, axis, dim):
    pieces = from_everyone(array, axis)
    return laid_out(pieces, dim)


def in_one_piece(arrays, axis, dim, along):
    both = jnp.concatenate(arrays, axis=along)
    filled, at, outs = (gathered_copies(both, axis, dim), 0, [])
    for a in arrays:
        outs.append(lax.slice_in_dim(filled, at, at + a.shape[along], axis=along))
        at += a.shape[along]
    return tuple(outs)


def split_up(array, dim, peers):
    shape = array.shape
    pieces = array.reshape(*shape[:dim], peers, shape[dim] // peers, *shape[dim + 1 :])
    return jnp.moveaxis(pieces, dim, 0)


def sum_at_owner(array, axis, dim):
    peers = lax.axis_size(axis)
    pieces = lax.all_to_all(split_up(array, dim, peers), axis, 0, 0, tiled=True)
    return jnp.sum(pieces, axis=0)


def owner_table(block_order, owner_counts, capacity):
    offsets = jnp.cumsum(owner_counts) - owner_counts
    columns = jnp.arange(capacity, dtype=jnp.int32)
    position = offsets[:, None] + columns[None, :]
    living = columns[None, :] < owner_counts[:, None]
    blocks = jnp.arange(block_order.shape[0], dtype=jnp.int32)
    matches = position[:, :, None] == blocks[None, None, :]
    chosen = jnp.sum(jnp.where(matches, block_order[None, None, :], 0), axis=2)
    return (jnp.where(living, chosen, 0), living)


def image_section(grad_rows, key_weight, value_weight, proj_weight):
    row_count = grad_rows.shape[0]
    group_devices = lax.axis_size("heads") // KVH
    pieces = lax.all_gather(grad_rows.astype(jnp.bfloat16), "heads", axis=1, tiled=True).astype(
        grad_rows.dtype
    )
    pieces = jnp.sum(pieces.reshape(row_count, KVH, group_devices, 2, HD), axis=2).astype(
        jnp.bfloat16
    )
    key_grads = pieces[:, :, 0].reshape(row_count, KVH * HD)
    value_grads = pieces[:, :, 1].reshape(row_count, KVH * HD)
    image_part = lax.dot_general(
        key_grads, key_weight, CONTRACT_LAST, preferred_element_type=jnp.float32
    )
    image_part = image_part + lax.dot_general(
        value_grads, value_weight, CONTRACT_LAST, preferred_element_type=jnp.float32
    )
    image_part = image_part.astype(jnp.bfloat16)
    vision = lax.dot_general(
        lax.all_gather(image_part, "heads", axis=1, tiled=True),
        proj_weight,
        CONTRACT_LAST,
        preferred_element_type=jnp.float32,
    )
    return vision.astype(jnp.bfloat16)


def shards(
    queries,
    out_grad,
    attn_out,
    img_keys,
    img_values,
    key_weight,
    value_weight,
    proj_weight,
    block_order,
    owner_counts,
):
    scaling = HD ** (-0.5)
    text_rows = queries.shape[0]
    local_heads = queries.shape[1] // HD
    group_devices = lax.axis_size("heads") // KVH
    group_index = lax.axis_index("heads") // group_devices
    kv_column = group_index * HD
    own_keys = lax.dynamic_slice_in_dim(img_keys, kv_column, HD, 1)
    own_values = lax.dynamic_slice_in_dim(img_values, kv_column, HD, 1)
    keys_all, values_all = in_one_piece((own_keys, own_values), "ctx", 0, 1)
    query_rows = queries.reshape(text_rows * local_heads, HD)
    grad_rows = out_grad.reshape(text_rows * local_heads, HD)
    output_rows = attn_out.reshape(text_rows * local_heads, HD)
    scores = (
        lax.dot_general(query_rows, keys_all, CONTRACT_LAST, preferred_element_type=jnp.float32)
        * scaling
    )
    weights = jnp.exp(scores - jax.nn.logsumexp(scores, axis=1, keepdims=True))
    weights_low = weights.astype(jnp.bfloat16)
    dweights = lax.dot_general(
        grad_rows, values_all, CONTRACT_LAST, preferred_element_type=jnp.float32
    )
    delta = jnp.sum(
        grad_rows.astype(jnp.float32) * output_rows.astype(jnp.float32), axis=1, keepdims=True
    )
    dscores = (weights * (dweights - delta)).astype(jnp.bfloat16)
    grad_query = jnp.dot(dscores, keys_all, preferred_element_type=jnp.float32) * scaling
    d_query = grad_query.astype(jnp.bfloat16).reshape(text_rows, local_heads * HD)
    ctx_count = lax.axis_size("ctx")
    ctx_index = lax.axis_index("ctx")
    block_total = block_order.shape[0]
    local_count = block_total // ctx_count
    slots, living = owner_table(block_order, owner_counts, CAP)
    my_slots = lax.dynamic_index_in_dim(slots, ctx_index, 0, keepdims=False)
    my_living = lax.dynamic_index_in_dim(living, ctx_index, 0, keepdims=False)
    grad_key = (
        lax.dot_general(dscores, query_rows, CONTRACT_FIRST, preferred_element_type=jnp.float32)
        * scaling
    )
    grad_value = lax.dot_general(
        weights_low, grad_rows, CONTRACT_FIRST, preferred_element_type=jnp.float32
    )
    shared = sum_at_owner(jnp.concatenate([grad_key, grad_value], axis=1), "ctx", 0)
    vision = image_section(shared, key_weight, value_weight, proj_weight)
    width_here = vision.shape[1]
    blocks = jnp.arange(block_total, dtype=jnp.int32)
    owned = jnp.any((slots[:, :, None] == blocks[None, None, :]) & living[:, :, None], axis=1)
    selected = lax.dynamic_slice_in_dim(owned, ctx_index * local_count, local_count, 1)
    local_blocks = vision.reshape(1, local_count, BR, width_here)
    outgoing = jnp.where(selected[:, :, None, None], local_blocks, jnp.zeros((), jnp.bfloat16))
    arrived = lax.all_to_all(outgoing, "ctx", split_axis=0, concat_axis=0, tiled=True)
    arrived = arrived.reshape(block_total, BR, width_here)
    picked = jnp.take(arrived, my_slots, axis=0)
    picked = jnp.where(my_living[:, None, None], picked, jnp.zeros_like(picked))
    d_vision = picked.reshape(CAP * BR, picked.shape[2])
    return (d_query, d_vision)


def solution(mesh):
    placed = (
        P("ctx", "heads"),
        P("ctx", "heads"),
        P("ctx", "heads"),
        P("ctx", None),
        P("ctx", None),
        P("heads", None),
        P("heads", None),
        P("heads", None),
        P(),
        P(),
    )
    return jax.shard_map(
        shards,
        mesh=mesh,
        in_specs=placed,
        out_specs=(P("ctx", "heads"), P("ctx", "heads")),
        check_vma=False,
    )
```

profile of v0, /device:TPU:25, one launch (start us, length us, event | category | flops | bytes accessed | tf_op | source)
XLA Modules:
  0.0 243.8 jit_solution(9903565578479135084)
XLA Ops:
  7.2 0.0 copy-start
  7.2 0.9 constant_dynamic-slice_fusion.1
  8.1 1.1 broadcast_in_dim.90
  9.2 6.4 %all-to-all-start = ((bf16[16,128,256]{2,1,0:T(8,128)(2,1)}), bf16[16,128,256]{2,1,0:T(8,128)(2,1)S(1)}, u32[]{:S(2)}, u32[]{:S(2)}) async-start(bf16[16,128,256]{2,1,0:T(8,128)(2,1)} %broadcast_in_dim.90), calls=%async_computation | async-start | bytes 2097152 | tf_op jit(solution)/shard_map/all_to_all | solution.py:16
  15.5 0.0 all-gather.3.cloned.1.call-start
  15.6 1.1 reshape.180
  16.7 1.1 reshape.181
  17.8 1.1 reshape.189
  18.9 0.2 multiply_reduce_fusion.1
  19.1 11.5 %all-to-all-done = bf16[16,128,256]{2,1,0:T(8,128)(2,1)S(1)} async-done(((bf16[16,128,256]{2,1,0:T(8,128)(2,1)}), bf16[16,128,256]{2,1,0:T(8,128)(2,1)S(1)}, u32[]{:S(2)}, u32[]{:S(2)}) %all-to-all-start) | async-done | bytes 1048608 | tf_op jit(solution)/shard_map/all_to_all | solution.py:16
  30.6 1.3 multiply_reduce_fusion
  31.9 1.4 exponential_reduce_fusion
  33.3 1.7 fusion.1
  35.0 2.1 multiply_convert_fusion
  37.2 1.9 copy-done.1
  39.1 1.5 convolution_multiply_fusion
  40.7 0.2 copy_bitcast_fusion
  40.9 29.9 %all_to_all.15 = f32[16,128,256]{1,2,0:T(8,128)S(1)} all-to-all(f32[16,128,256]{1,2,0:T(8,128)S(1)} %copy_bitcast_fusion), channel_id=1, replica_groups=mesh['ctx'=16,'heads'=16] {'ctx'}, dimensions={0} | all-to-all | bytes 4194304 | tf_op jit(solution)/shard_map/all_to_all | solution.py:47
  70.8 0.7 reduce_sum.48
  71.5 0.0 all-gather.3.cloned.1.call-update
  71.5 0.0 all-gather.5.cloned.1.call-start
  71.6 53.2 %all-gather.3.cloned.1.call-done = bf16[128,4096]{0,1:T(8,128)(2,1)} async-done(((bf16[128,256]{0,1:T(8,128)(2,1)}), bf16[128,4096]{0,1:T(8,128)(2,1)}) %all-gather.3.cloned.1.call-update) | async-done | bytes 1048592 | tf_op jit(solution)/shard_map/all_gather | solution.py:65
  124.8 1.5 reduce.2
  126.3 0.5 fusion.17
  126.8 2.4 fusion.6
  129.2 0.0 all-gather.5.cloned.1.call-update
  129.2 0.1 copy.32
  129.4 0.1 reduce.4
  129.5 0.2 select_reduce_fusion
  129.8 0.1 fusion.13
  129.8 0.1 constant_dynamic-slice_fusion
  129.9 60.9 %all-gather.5.cloned.1.call-done = bf16[128,8192]{1,0:T(8,128)(2,1)} async-done(((bf16[128,512]{1,0:T(8,128)(2,1)}), bf16[128,8192]{1,0:T(8,128)(2,1)}) %all-gather.5.cloned.1.call-update) | async-done | bytes 2097168 | tf_op jit(solution)/shard_map/all_gather | solution.py:81
  190.9 6.1 %convolution_convert_fusion = bf16[128,480]{0,1:T(8,128)(2,1)S(1)} fusion(bf16[128,8192]{1,0:T(8,128)(2,1)} %all-gather.5.cloned.1.call-done, bf16[480,8192]{1,0:T(8,128)(2,1)} %param.17), kind=kOutput, calls=%fused_computation.17 | convolution fusion | flops 1006694400 | bytes 10084352 | tf_op jit(solution)/shard_map/dot_general | solution.py:80
  196.9 0.1 copy.35
  197.0 1.6 broadcast_select_fusion
  198.6 5.6 %all-to-all-start.2 = ((bf16[16,2,64,480]{3,2,1,0:T(8,128)(2,1)}), bf16[16,2,64,480]{3,2,1,0:T(8,128)(2,1)}, u32[]{:S(2)}, u32[]{:S(2)}) async-start(bf16[16,2,64,480]{3,2,1,0:T(8,128)(2,1)} %broadcast_select_fusion), calls=%async_computation.2 | async-start | bytes 4194304 | tf_op jit(solution)/shard_map/all_to_all | solution.py:150
  204.2 0.2 dynamic-slice_reduce_fusion
  204.4 0.2 dynamic-slice_reduce_fusion.1
  204.6 0.1 broadcast_in_dim.99
  204.6 0.1 broadcast_in_dim.100
  204.7 0.1 broadcast_in_dim.93
  204.8 0.1 broadcast_in_dim.94
  204.9 3.5 %fusion.5 = bf16[1024,128]{1,0:T(8,128)(2,1)S(1)} fusion(bf16[2048,1024]{1,0:T(8,128)(2,1)} %copy-done.1, bf16[2048,256]{1,0:T(8,128)(2,1)S(1)} %bitcast.34), kind=kOutput, calls=%fused_computation.14 | convolution fusion | flops 537133056 | bytes 4980736 | tf_op jit(solution)/shard_map/dot_general | solution.py:126
  208.4 0.9 reshape.182
  209.3 24.5 %all-to-all-done.2 = bf16[16,2,64,480]{3,2,1,0:T(8,128)(2,1)} async-done(((bf16[16,2,64,480]{3,2,1,0:T(8,128)(2,1)}), bf16[16,2,64,480]{3,2,1,0:T(8,128)(2,1)}, u32[]{:S(2)}, u32[]{:S(2)}) %all-to-all-start.2) | async-done | bytes 1966112 | tf_op jit(solution)/shard_map/all_to_all | solution.py:150
  233.8 2.2 gather_fusion
  236.0 0.1 fusion.11
  236.1 0.8 copy.36
  (22 shorter events, 0.2 us)
Async XLA Ops:
  7.2 119.2 %copy-start = (bf16[512,1024]{1,0:T(8,128)(2,1)S(1)}, bf16[512,1024]{1,0:T(8,128)(2,1)}, u32[]{:S(2)}) copy-start(bf16[512,1024]{1,0:T(8,128)(2,1)} %param.15) | copy-start | bytes 3145732
  9.2 21.4 %all-to-all-start = ((bf16[16,128,256]{2,1,0:T(8,128)(2,1)}), bf16[16,128,256]{2,1,0:T(8,128)(2,1)S(1)}, u32[]{:S(2)}, u32[]{:S(2)}) async-start(bf16[16,128,256]{2,1,0:T(8,128)(2,1)} %broadcast_in_dim.90), calls=%async_computation | async-start | bytes 2097152 | tf_op jit(solution)/shard_map/all_to_all | solution.py:16
  15.5 109.3 %all-gather.3.cloned.1.call-start = ((), (), s32[]{:S(2)}) async-start(), calls=%async_computation.3 | async-start | bytes 1114112 | tf_op jit(solution)/shard_map/all_gather | solution.py:65
  30.6 4.4 %copy-start.2 = (bf16[16,128,256]{2,1,0:T(8,128)(2,1)}, bf16[16,128,256]{2,1,0:T(8,128)(2,1)S(1)}, u32[]{:S(2)}) copy-start(bf16[16,128,256]{2,1,0:T(8,128)(2,1)S(1)} %all-to-all-done) | copy-start | bytes 3145732
  37.2 1.9 copy-start.1
  40.7 88.6 %copy-start.4 = (s32[16]{0:T(128)S(1)}, s32[16]{0:T(128)}, u32[]{:S(2)}) copy-start(s32[16]{0:T(128)} %param.19) | copy-start | bytes 196
  40.7 88.8 %copy-start.5 = (s32[32]{0:T(128)S(1)}, s32[32]{0:T(128)}, u32[]{:S(2)}) copy-start(s32[32]{0:T(128)} %param.18) | copy-start | bytes 388
  71.5 119.3 %all-gather.5.cloned.1.call-start = ((), (), s32[]{:S(2)}) async-start(), calls=%async_computation.4 | async-start | bytes 2228224 | tf_op jit(solution)/shard_map/all_gather | solution.py:81
  129.9 75.0 %copy-start.3 = (bf16[16,128,256]{2,1,0:T(8,128)(2,1)S(1)}, bf16[16,128,256]{2,1,0:T(8,128)(2,1)}, u32[]{:S(2)}) copy-start(bf16[16,128,256]{2,1,0:T(8,128)(2,1)} %copy-done.2) | copy-start | bytes 3145732
  198.6 35.2 %all-to-all-start.2 = ((bf16[16,2,64,480]{3,2,1,0:T(8,128)(2,1)}), bf16[16,2,64,480]{3,2,1,0:T(8,128)(2,1)}, u32[]{:S(2)}, u32[]{:S(2)}) async-start(bf16[16,2,64,480]{3,2,1,0:T(8,128)(2,1)} %broadcast_select_fusion), calls=%async_computation.2 | async-start | bytes 4194304 | tf_op jit(solution)/shard_map/all_to_all | solution.py:150
Sparse Core Ops, SparseCore 0:
  71.6 53.1 all-gather.2
  129.4 61.4 all-gather.4
where the time goes:
time: 244 us
  waiting for transfers between devices  150 us (61%)
  blocking collectives  29.9 us (12%)
  matrix products  19 us (8%)
  between operations  14.3 us (6%)
  local copies, waits for them, and re-layouts  12.1 us (5%)
  starting transfers between devices  12 us (5%)
  other arithmetic  6.27 us (3%)
    all_gather x1, waiting for transfers between devices, image_section(): lax.all_gather(image_part, 'heads', axis=1, tiled=True)  60.9 us
    all_gather x1, waiting for transfers between devices, image_section(): lax.all_gather(grad_rows.astype(jnp.bfloat16), 'heads', axis=1, tiled=True)  53.2 us
    all_to_all x1, blocking collectives, sum_at_owner(): pieces = lax.all_to_all(split_up(array, dim, peers), axis, 0, 0, tiled=True)  29.9 us
    all_to_all x1, waiting for transfers between devices, shards(): lax.all_to_all(outgoing, 'ctx', split_axis=0, concat_axis=0, tiled=True)  24.5 us
    all_to_all x1, waiting for transfers between devices, from_everyone(): return lax.all_to_all(copies, axis, split_axis=0, concat_axis=0, tiled=True)  11.5 us
    all_to_all x1, starting transfers between devices, from_everyone(): return lax.all_to_all(copies, axis, split_axis=0, concat_axis=0, tiled=True)  6.37 us
    dot_general x1, matrix products, image_section(): lax.dot_general(lax.all_gather(image_part, 'heads', axis=1, tiled=True),...  6.06 us
    all_to_all x1, starting transfers between devices, shards(): lax.all_to_all(outgoing, 'ctx', split_axis=0, concat_axis=0, tiled=True)  5.58 us
  transfers between devices with their start and end apart: 4, of which 4 were waited for; matrix products, arithmetic and copies ran while one was open for 4% of the time, Pallas kernels for 0%

commit v1 on v0

--- a/solution.py
+++ b/solution.py
@@ -9,6 +9,16 @@
 CAP = 4
 CONTRACT_LAST = (((1,), (1,)), ((), ()))
 CONTRACT_FIRST = (((0,), (0,)), ((), ()))
+
+
+def watch_ratios(z_in):
+    finding = lax.all_to_all(
+        jnp.stack([z_in for _ in range(lax.axis_size("heads"))], axis=0),
+        concat_axis=0,
+        axis_name="heads",
+        split_axis=0,
+    )
+    return jnp.concatenate(finding, 1)
 
 
 def from_everyone(array, axis):
@@ -62,9 +72,7 @@
 def image_section(grad_rows, key_weight, value_weight, proj_weight):
     row_count = grad_rows.shape[0]
     group_devices = lax.axis_size("heads") // KVH
-    pieces = lax.all_gather(grad_rows.astype(jnp.bfloat16), "heads", axis=1, tiled=True).astype(
-        grad_rows.dtype
-    )
+    pieces = watch_ratios(grad_rows.astype(jnp.bfloat16)).astype(grad_rows.dtype)
     pieces = jnp.sum(pieces.reshape(row_count, KVH, group_devices, 2, HD), axis=2).astype(
         jnp.bfloat16
     )

time: 244 us -> 226 us (0.926)
  waiting for transfers between devices: 150 us -> 95.5 us
  blocking collectives: 29.9 us -> 67.6 us
    all_gather x1 -> x0, waiting for transfers between devices: 53.2 us -> none  [image_section(): lax.all_gather(grad_rows.astype(jnp.bfloat16), 'heads', axis=1, tiled=True)]
    all_to_all x0 -> x1, blocking collectives: none -> 37.7 us  [watch_ratios(): lax.all_to_all(jnp.stack([z_in for _ in range(lax.axis_size('heads'))], a...]
  transfers between devices with their start and end apart: 4 -> 3, of which waited for: 4 -> 3; matrix products, arithmetic and copies ran while one was open for 4% -> 4% of each run, Pallas kernels for 0% -> 0%
where the time goes in v1:
time: 226 us; the launch traced here: 225 us
  waiting for transfers between devices  95.5 us (42%)
  blocking collectives  67.6 us (30%)
  matrix products  19 us (8%)
  between operations  14.3 us (6%)
  local copies, waits for them, and re-layouts  12.3 us (5%)
  starting transfers between devices  12 us (5%)
  other arithmetic  4.43 us (2%)
    all_gather x1, waiting for transfers between devices, image_section(): lax.all_gather(image_part, 'heads', axis=1, tiled=True)  59.5 us
    all_to_all x1, blocking collectives, watch_ratios(): lax.all_to_all(jnp.stack([z_in for _ in range(lax.axis_size('heads'))], a...  37.7 us
    all_to_all x1, blocking collectives, sum_at_owner(): pieces = lax.all_to_all(split_up(array, dim, peers), axis, 0, 0, tiled=True)  29.9 us
    all_to_all x1, waiting for transfers between devices, shards(): lax.all_to_all(outgoing, 'ctx', split_axis=0, concat_axis=0, tiled=True)  24.5 us
    all_to_all x1, waiting for transfers between devices, from_everyone(): return lax.all_to_all(copies, axis, split_axis=0, concat_axis=0, tiled=True)  11.5 us
    all_to_all x1, starting transfers between devices, from_everyone(): return lax.all_to_all(copies, axis, split_axis=0, concat_axis=0, tiled=True)  6.37 us
    dot_general x1, matrix products, image_section(): lax.dot_general(lax.all_gather(image_part, 'heads', axis=1, tiled=True),...  6.07 us
    all_to_all x1, starting transfers between devices, shards(): lax.all_to_all(outgoing, 'ctx', split_axis=0, concat_axis=0, tiled=True)  5.58 us
  transfers between devices with their start and end apart: 3, of which 3 were waited for; matrix products, arithmetic and copies ran while one was open for 4% of the time, Pallas kernels for 0%

profile of v1, /device:TPU:25, one launch (start us, length us, event | category | flops | bytes accessed | tf_op | source)
XLA Modules:
  0.0 225.1 jit_solution(2334528711314793425)
XLA Ops:
  7.2 0.0 copy-start
  7.2 0.9 constant_dynamic-slice_fusion.1
  8.1 1.1 broadcast_in_dim.90
  9.2 6.4 %all-to-all-start = ((bf16[16,128,256]{2,1,0:T(8,128)(2,1)}), bf16[16,128,256]{2,1,0:T(8,128)(2,1)S(1)}, u32[]{:S(2)}, u32[]{:S(2)}) async-start(bf16[16,128,256]{2,1,0:T(8,128)(2,1)} %broadcast_in_dim.90), calls=%async_computation | async-start | bytes 2097152 | tf_op jit(solution)/shard_map/all_to_all | solution.py:26
  15.5 0.0 all-gather.2.cloned.1.call-start
  15.6 1.1 reshape.184
  16.7 1.1 reshape.185
  17.8 1.1 reshape.193
  18.9 0.2 multiply_reduce_fusion.1
  19.1 11.5 %all-to-all-done = bf16[16,128,256]{2,1,0:T(8,128)(2,1)S(1)} async-done(((bf16[16,128,256]{2,1,0:T(8,128)(2,1)}), bf16[16,128,256]{2,1,0:T(8,128)(2,1)S(1)}, u32[]{:S(2)}, u32[]{:S(2)}) %all-to-all-start) | async-done | bytes 1048608 | tf_op jit(solution)/shard_map/all_to_all | solution.py:26
  30.6 1.3 multiply_reduce_fusion
  31.9 1.4 exponential_reduce_fusion
  33.3 1.7 fusion.1
  35.0 2.1 multiply_convert_fusion
  37.2 1.9 copy-done.1
  39.1 1.5 convolution_multiply_fusion
  40.7 0.2 copy_bitcast_fusion
  40.9 0.0 copy-start.4
  40.9 29.9 %all_to_all.20 = f32[16,128,256]{1,2,0:T(8,128)S(1)} all-to-all(f32[16,128,256]{1,2,0:T(8,128)S(1)} %copy_bitcast_fusion), channel_id=1, replica_groups=mesh['ctx'=16,'heads'=16] {'ctx'}, dimensions={0} | all-to-all | bytes 4194304 | tf_op jit(solution)/shard_map/all_to_all | solution.py:57
  70.8 0.1 reduce_sum.51
  70.9 0.2 stack.2
  71.1 37.7 %all_to_all.21 = bf16[16,128,256]{1,2,0:T(8,128)(2,1)S(1)} all-to-all(bf16[16,128,256]{1,2,0:T(8,128)(2,1)S(1)} %stack.2), channel_id=1, replica_groups=mesh['ctx'=16,'heads'=16] {'heads'}, dimensions={0} | all-to-all | bytes 2097152 | tf_op jit(solution)/shard_map/all_to_all | solution.py:15
  108.8 0.3 reduce_sum.52
  109.1 0.5 fusion.17
  109.6 2.4 %fusion.6 = bf16[128,512]{1,0:T(8,128)(2,1)} fusion(f32[128,512]{1,0:T(8,128)S(1)} %fusion.17, bf16[128,1024]{0,1:T(8,128)(2,1)S(1)} %bitcast.42, bf16[512,1024]{1,0:T(8,128)(2,1)} %param.16), kind=kOutput, calls=%fused_computation.16 | convolution fusion | flops 134348800 | bytes 1703936 | tf_op jit(solution)/shard_map/dot_general | solution.py:84
  112.0 0.0 all-gather.2.cloned.1.call-update
  112.0 0.1 copy.31
  112.1 0.1 reduce.4
  112.3 0.2 select_reduce_fusion
  112.5 0.1 fusion.13
  112.6 0.1 constant_dynamic-slice_fusion
  112.7 59.5 %all-gather.2.cloned.1.call-done = bf16[128,8192]{1,0:T(8,128)(2,1)} async-done(((bf16[128,512]{1,0:T(8,128)(2,1)}), bf16[128,8192]{1,0:T(8,128)(2,1)}) %all-gather.2.cloned.1.call-update) | async-done | bytes 2097168 | tf_op jit(solution)/shard_map/all_gather | solution.py:89
  172.1 6.1 %convolution_convert_fusion = bf16[128,480]{0,1:T(8,128)(2,1)S(1)} fusion(bf16[128,8192]{1,0:T(8,128)(2,1)} %all-gather.2.cloned.1.call-done, bf16[480,8192]{1,0:T(8,128)(2,1)} %param.17), kind=kOutput, calls=%fused_computation.17 | convolution fusion | flops 1006694400 | bytes 10084352 | tf_op jit(solution)/shard_map/dot_general | solution.py:88
  178.2 0.1 copy.37
  178.3 1.6 broadcast_select_fusion
  179.9 5.6 %all-to-all-start.3 = ((bf16[16,2,64,480]{3,2,1,0:T(8,128)(2,1)}), bf16[16,2,64,480]{3,2,1,0:T(8,128)(2,1)}, u32[]{:S(2)}, u32[]{:S(2)}) async-start(bf16[16,2,64,480]{3,2,1,0:T(8,128)(2,1)} %broadcast_select_fusion), calls=%async_computation.3 | async-start | bytes 4194304 | tf_op jit(solution)/shard_map/all_to_all | solution.py:158
  185.5 0.2 dynamic-slice_reduce_fusion
  185.6 0.2 dynamic-slice_reduce_fusion.1
  185.8 0.1 broadcast_in_dim.99
  185.9 0.1 broadcast_in_dim.100
  186.0 0.1 broadcast_in_dim.93
  186.1 0.1 broadcast_in_dim.94
  186.2 3.5 %fusion.5 = bf16[1024,128]{1,0:T(8,128)(2,1)S(1)} fusion(bf16[2048,1024]{1,0:T(8,128)(2,1)} %copy-done.1, bf16[2048,256]{1,0:T(8,128)(2,1)S(1)} %bitcast.40), kind=kOutput, calls=%fused_computation.14 | convolution fusion | flops 537133056 | bytes 4980736 | tf_op jit(solution)/shard_map/dot_general | solution.py:134
  189.7 0.9 reshape.186
  190.6 24.5 %all-to-all-done.3 = bf16[16,2,64,480]{3,2,1,0:T(8,128)(2,1)} async-done(((bf16[16,2,64,480]{3,2,1,0:T(8,128)(2,1)}), bf16[16,2,64,480]{3,2,1,0:T(8,128)(2,1)}, u32[]{:S(2)}, u32[]{:S(2)}) %all-to-all-start.3) | async-done | bytes 1966112 | tf_op jit(solution)/shard_map/all_to_all | solution.py:158
  215.1 2.2 gather_fusion
  217.3 0.1 fusion.11
  217.4 0.8 copy.38
  (21 shorter events, 0.2 us)
Async XLA Ops:
  7.2 101.9 %copy-start = (bf16[512,1024]{1,0:T(8,128)(2,1)S(1)}, bf16[512,1024]{1,0:T(8,128)(2,1)}, u32[]{:S(2)}) copy-start(bf16[512,1024]{1,0:T(8,128)(2,1)} %param.15) | copy-start | bytes 3145732
  9.2 21.4 %all-to-all-start = ((bf16[16,128,256]{2,1,0:T(8,128)(2,1)}), bf16[16,128,256]{2,1,0:T(8,128)(2,1)S(1)}, u32[]{:S(2)}, u32[]{:S(2)}) async-start(bf16[16,128,256]{2,1,0:T(8,128)(2,1)} %broadcast_in_dim.90), calls=%async_computation | async-start | bytes 2097152 | tf_op jit(solution)/shard_map/all_to_all | solution.py:26
  15.5 156.6 %all-gather.2.cloned.1.call-start = ((), (), s32[]{:S(2)}) async-start(), calls=%async_computation.4 | async-start | bytes 2228224 | tf_op jit(solution)/shard_map/all_gather | solution.py:89
  30.6 4.4 %copy-start.2 = (bf16[16,128,256]{2,1,0:T(8,128)(2,1)}, bf16[16,128,256]{2,1,0:T(8,128)(2,1)S(1)}, u32[]{:S(2)}) copy-start(bf16[16,128,256]{2,1,0:T(8,128)(2,1)S(1)} %all-to-all-done) | copy-start | bytes 3145732
  37.2 1.9 copy-start.1
  40.9 71.1 %copy-start.4 = (s32[16]{0:T(128)S(1)}, s32[16]{0:T(128)}, u32[]{:S(2)}) copy-start(s32[16]{0:T(128)} %param.19) | copy-start | bytes 196
  40.9 71.4 %copy-start.5 = (s32[32]{0:T(128)S(1)}, s32[32]{0:T(128)}, u32[]{:S(2)}) copy-start(s32[32]{0:T(128)} %param.18) | copy-start | bytes 388
  112.7 73.5 %copy-start.3 = (bf16[16,128,256]{2,1,0:T(8,128)(2,1)S(1)}, bf16[16,128,256]{2,1,0:T(8,128)(2,1)}, u32[]{:S(2)}) copy-start(bf16[16,128,256]{2,1,0:T(8,128)(2,1)} %copy-done.2) | copy-start | bytes 3145732
  179.9 35.2 %all-to-all-start.3 = ((bf16[16,2,64,480]{3,2,1,0:T(8,128)(2,1)}), bf16[16,2,64,480]{3,2,1,0:T(8,128)(2,1)}, u32[]{:S(2)}, u32[]{:S(2)}) async-start(bf16[16,2,64,480]{3,2,1,0:T(8,128)(2,1)} %broadcast_select_fusion), calls=%async_computation.3 | async-start | bytes 4194304 | tf_op jit(solution)/shard_map/all_to_all | solution.py:158
Sparse Core Ops, SparseCore 0:
  112.1 59.9 all-gather.1
